TPU v7x, 32 devices: a whole 2x2x4 slice. The times are simulated.
32 devices in a mesh: groups: 2 (over y), dp: 16 (over z, x, core).
Axes of the slice: x: 2, y: 2, z: 4, core: 2. Of those that a mesh axis runs over, the one named last changes fastest.
Arguments:
- state: bfloat16 [32, 128, 64, 128], P(('groups', 'dp')), parts along dimension 0, may hold values from -6 to 6
- x_in: bfloat16 [32, 8192], P(('groups', 'dp')), parts along dimension 0, may hold values from -6 to 6
- z_gate: bfloat16 [32, 8192], P(('groups', 'dp')), parts along dimension 0, may hold values from -6 to 6
- b_in: bfloat16 [32, 512], P(('groups', 'dp')), parts along dimension 0, may hold values from -6 to 6
- c_in: bfloat16 [32, 512], P(('groups', 'dp')), parts along dimension 0, may hold values from -0.59765625 to 0.59765625
- dt_raw: float32 [32, 128], P(('groups', 'dp')), parts along dimension 0, may hold values from -5 to 5
- dt_bias: float32 [128], replicated, may hold values from -3 to 0.5
- a_log: float32 [128], replicated, may hold values from -1 to 1.5
- d_skip: float32 [128], replicated, may hold values from 0.3 to 1.7
- norm_gain: float32 [8192], replicated, may hold values from 0.1 to 1.9
- out_proj: bfloat16 [8192, 8192], P('dp'), may hold values from -0.0625 to 0.0625
- active: int32 [32], P(('groups', 'dp')), parts along dimension 0, may hold values from 0 to 1
- plan: int32 [16, 2], P('groups'), parts along dimension 0, may hold values from 0 to 15, as said below
Outputs:
- mixed: bfloat16 [32, 8192], P(('groups', 'dp')), parts along dimension 0
- new_state: bfloat16 [32, 128, 64, 128], P(('groups', 'dp')), parts along dimension 0
There are 2 independent parts, one for each index of `groups`. A program takes and returns all parts, laid end to end along the dimension named above; an argument that names none is the same for every part. Nothing has to cross between parts.
Inputs may be any that keep to these rules, and one draw needn't show every extreme that they name: `plan`: exactly 8 moves. Source slots are distinct and live in active; destination slots are distinct and not live in active. Slot k belongs to device k. Each device holds the source of at most one move and the destination of at most one, never both; both bounds are reached.
All inputs are finite; a program needn't handle non-finite values.
Results may differ from a plain program's by a relative error of at most 0.0049.
Values may be sent and summed in bfloat16 or wider, within the bound.
No kernel may reach another device: no remote copies, remote signals or barrier semaphores. Data moves between devices by JAX's collectives and lax.ppermute only.
A program may use at most 64 MiB of HBM per device.

v0:
```python
import jax
import jax.numpy as jnp
from jax import lax
from jax.sharding import PartitionSpec as P

H = 128
P_SIZE = 64
N = 128
G = 4


def update_row(st, xr, zr, br, cr, dtr, dt_bias, a_log, d_skip, norm_gain):
    step_size = jax.nn.softplus(dtr + dt_bias)
    decay = jnp.exp(-jnp.exp(a_log) * step_size)
    inputs = xr.astype(jnp.float32).reshape(H, P_SIZE)
    b_heads = jnp.repeat(br.astype(jnp.float32).reshape(G, N), H // G, axis=0)
    c_heads = jnp.repeat(cr.astype(jnp.float32).reshape(G, N), H // G, axis=0)
    fresh = (
        decay[:, None, None] * st.astype(jnp.float32)
        + (step_size[:, None] * inputs)[:, :, None] * b_heads[:, None, :]
    )
    y_out = jnp.sum(fresh * c_heads[:, None, :], axis=2) + d_skip[:, None] * inputs
    gated = (y_out.reshape(-1) * jax.nn.silu(zr.astype(jnp.float32))).reshape(G, -1)
    factor = lax.rsqrt(jnp.mean(gated * gated, axis=1, keepdims=True) + 1e-05)
    normed = ((gated * factor).reshape(-1) * norm_gain).astype(jnp.bfloat16)
    return (fresh.astype(jnp.bfloat16), normed)


def local(
    state,
    x_in,
    z_gate,
    b_in,
    c_in,
    dt_raw,
    dt_bias,
    a_log,
    d_skip,
    norm_gain,
    out_proj,
    active,
    plan,
):
    slots = state.shape[0]
    devices = lax.axis_size("dp")
    myself = lax.axis_index("dp")
    first_slot = myself * slots
    source = plan[:, 0]
    target = plan[:, 1]
    source_dev = source // slots
    target_dev = target // slots
    slot_ids = jnp.arange(slots, dtype=jnp.int32)
    sends = source_dev == myself
    outgoing = state
    outgoing = jnp.where(jnp.any(sends), outgoing, jnp.zeros((), state.dtype))
    device_ids = jnp.arange(devices, dtype=jnp.int32)
    matches = target_dev[:, None] == device_ids[None, :]
    sender_of = jnp.sum(jnp.where(matches, source_dev[:, None], 0), axis=0)
    has_sender = jnp.any(matches, axis=0)
    head_view = lax.all_to_all(outgoing, "dp", split_axis=1, concat_axis=0, tiled=True)
    routed = jnp.take(head_view, sender_of, axis=0)
    arrived = lax.all_to_all(
        jnp.where(has_sender[:, None, None, None], routed, jnp.zeros((), state.dtype)),
        "dp",
        split_axis=0,
        concat_axis=1,
        tiled=True,
    )
    receives = target_dev == myself
    recv_slot = jnp.sum(jnp.where(receives, target - first_slot, 0))
    chosen = (slot_ids == recv_slot) & jnp.any(receives)
    placed = jnp.where(chosen[:, None, None, None], arrived, state)
    global_ids = first_slot + slot_ids
    leaving = jnp.any(source[None, :] == global_ids[:, None], axis=1)
    coming = jnp.any(target[None, :] == global_ids[:, None], axis=1)
    live = jnp.where(leaving, 0, jnp.where(coming, 1, active))

    def one_row(st, xr, zr, br, cr, dtr):
        return update_row(st, xr, zr, br, cr, dtr, dt_bias, a_log, d_skip, norm_gain)

    fresh, normed = jax.vmap(one_row)(placed, x_in, z_gate, b_in, c_in, dt_raw)
    normed = jnp.where(live[:, None] > 0, normed, jnp.zeros((), jnp.bfloat16))
    new_state = jnp.where(live[:, None, None, None] > 0, fresh, jnp.zeros((), jnp.bfloat16))
    head_cols = lax.all_to_all(normed, "dp", split_axis=1, concat_axis=0, tiled=True)
    mixed = lax.psum_scatter(
        jnp.dot(head_cols, out_proj, preferred_element_type=jnp.float32),
        "dp",
        scatter_dimension=0,
        tiled=True,
    ).astype(jnp.bfloat16)
    return (mixed, new_state)


def solution(mesh):
    in_specs = (
        P(("groups", "dp"), None, None, None),
        P(("groups", "dp"), None),
        P(("groups", "dp"), None),
        P(("groups", "dp"), None),
        P(("groups", "dp"), None),
        P(("groups", "dp"), None),
        P(),
        P(),
        P(),
        P(),
        P("dp", None),
        P(("groups", "dp")),
        P("groups", None),
    )
    out_specs = (P(("groups", "dp"), None), P(("groups", "dp"), None, None, None))
    return jax.shard_map(local, mesh=mesh, in_specs=in_specs, out_specs=out_specs, check_vma=False)
```

profile of v0, /device:TPU:0, one launch (start us, length us, event | category | flops | bytes accessed | tf_op | source)
XLA Modules:
  0.0 208.8 jit_solution(6131589197692125429)
XLA Ops:
  0.6 1.5 compare_reduce_fusion.3
  2.1 3.7 %bitcast_select_fusion.1 = bf16[1,128,64,128]{3,2,0,1:T(8,128)(2,1)} fusion(bf16[1,128,64,128]{3,2,1,0:T(8,128)(2,1)} %param.13, pred[]{:T(512)} %get-tuple-element.11), kind=kLoop, calls=%fused_computation.7 | loop fusion | flops 1048576 | bytes 4194305 | tf_op jit(solution)/shard_map/jit(_where)/select_n | solution.py:55
  5.9 7.5 %all-to-all-start = ((bf16[1,128,64,128]{3,2,0,1:T(8,128)(2,1)}), bf16[1,128,64,128]{3,2,0,1:T(8,128)(2,1)S(1)}, u32[]{:S(2)}, u32[]{:S(2)}) async-start(bf16[1,128,64,128]{3,2,0,1:T(8,128)(2,1)} %bitcast_select_fusion.1), calls=%async_computation | async-start | bytes 4194304 | tf_op jit(solution)/shard_map/all_to_all | solution.py:60
  13.4 0.0 copy-done.5
  13.4 0.1 select_reduce_fusion
  13.5 0.1 fusion.8
  13.6 40.8 %all-to-all-done = bf16[1,128,64,128]{3,2,0,1:T(8,128)(2,1)S(1)} async-done(((bf16[1,128,64,128]{3,2,0,1:T(8,128)(2,1)}), bf16[1,128,64,128]{3,2,0,1:T(8,128)(2,1)S(1)}, u32[]{:S(2)}, u32[]{:S(2)}) %all-to-all-start) | async-done | bytes 2097184 | tf_op jit(solution)/shard_map/all_to_all | solution.py:60
  54.4 1.3 copy-done.1
  55.7 2.5 %gather_fusion = bf16[16,8,64,128]{3,2,1,0:T(8,128)(2,1)S(1)} fusion(bf16[16,8,64,128]{3,2,1,0:T(8,128)(2,1)} %bitcast.59, s32[1024]{0:T(1024)S(1)} %pad_clamp_fusion), kind=kCustom, calls=%fused_computation | custom fusion | bytes 4194368 | tf_op jit(solution)/shard_map/jit(_take)/gather | solution.py:61
  58.2 1.6 select_select_fusion
  59.9 0.0 copy-start.12
  59.9 0.0 copy-start.9
  59.9 0.0 copy-start.10
  59.9 0.0 copy-start.11
  59.9 0.0 copy-start
  59.9 11.4 %all-to-all-start.1 = ((bf16[16,8,64,128]{3,2,1,0:T(8,128)(2,1)}), bf16[16,8,64,128]{3,2,1,0:T(8,128)(2,1)}, u32[]{:S(2)}, u32[]{:S(2)}) async-start(bf16[16,8,64,128]{3,2,1,0:T(8,128)(2,1)} %select_select_fusion), calls=%async_computation.1 | async-start | bytes 4194304 | tf_op jit(solution)/shard_map/all_to_all | solution.py:62
  71.3 0.0 copy-done.2
  71.3 0.1 convert_reduce_fusion
  71.4 0.1 reshape.216
  71.5 0.0 copy-done.6
  71.5 0.0 copy-done.7
  71.5 0.0 copy-done.8
  71.6 0.1 mul.124
  71.6 0.1 mul.125
  72.4 0.7 compare_reduce_fusion.1
  74.3 0.7 fusion.9
  76.2 0.0 copy-done.12
  76.2 0.6 dynamic-slice
  76.9 0.0 copy-done.9
  76.9 0.0 copy-done.10
  76.9 0.1 broadcast_multiply_fusion
  77.0 35.4 %all-to-all-done.1 = bf16[16,8,64,128]{3,2,1,0:T(8,128)(2,1)} async-done(((bf16[16,8,64,128]{3,2,1,0:T(8,128)(2,1)}), bf16[16,8,64,128]{3,2,1,0:T(8,128)(2,1)}, u32[]{:S(2)}, u32[]{:S(2)}) %all-to-all-start.1) | async-done | bytes 2097184 | tf_op jit(solution)/shard_map/all_to_all | solution.py:62
  112.4 0.0 copy-start.4
  112.4 0.0 copy-start.3
  112.4 3.7 %multiply_reduce_fusion = f32[128,64]{1,0:T(8,128)S(1)} fusion(f32[128,128]{1,0:T(8,128)S(1)} %bitcast.62, f32[128,128]{1,0:T(8,128)S(1)} %bitcast.60, f32[128,64]{1,0:T(8,128)S(1)} %broadcast_multiply_fusion, f32[128]{0:T(128)S(1)} %get-tuple-element.14, bf16[1,128,64,128]{3,2,0,1:T(8,128)(2,1)} %bitcast.12, bf16[1,128,64,128]{3,2,1,0:T(8,128)(2,1)S(1)} %copy-done, ...), kind=kLoop, calls=%fused_computation.1 | loop fusion | flops 7331840 | bytes 4391425 | tf_op jit(solution)/shard_map/vmap()/reduce_sum | solution.py:22
  116.1 0.1 reduce_sum.44
  116.2 0.2 multiply_reduce_fusion.1
  116.4 0.1 reduce_sum.45
  116.6 0.1 mul.131
  116.7 0.5 broadcast.178
  117.2 0.7 reduce.15
  118.0 0.6 reshape.247
  118.6 12.3 %all-to-all-start.2 = ((bf16[16,2,256]{2,1,0:T(2,128)(2,1)}), bf16[16,2,256]{2,1,0:T(2,128)(2,1)S(1)}, u32[]{:S(2)}, u32[]{:S(2)}) async-start(bf16[16,2,256]{2,1,0:T(2,128)(2,1)} %reshape.247), calls=%async_computation.2 | async-start | bytes 32768 | tf_op jit(solution)/shard_map/all_to_all | solution.py:84
  130.9 4.8 %fusion.2 = bf16[1,128,64,128]{3,2,1,0:T(8,128)(2,1)} fusion(f32[128,128]{1,0:T(8,128)S(1)} %bitcast.61, f32[128,64]{1,0:T(8,128)S(1)} %broadcast_multiply_fusion, f32[128]{0:T(128)S(1)} %get-tuple-element.14, pred[]{:T(512)} %bitcast.2, bf16[1,128,64,128]{3,2,1,0:T(8,128)(2,1)S(1)} %copy-done, pred[]{:T(512)S(6)} %and.22, ...), kind=kLoop, calls=%fused_computation.5 | loop fusion | flops 7340032 | bytes 6390274
  135.7 1.7 all-to-all-done.2
  137.4 4.6 %fusion.5 = f32[16,8192]{1,0:T(8,128)S(1)} fusion(bf16[512,8192]{1,0:T(8,128)(2,1)} %param.23, bf16[1,16,512]{2,0,1:T(2,128)(2,1)S(1)} %bitcast.66), kind=kOutput, calls=%fused_computation.17 | convolution fusion | flops 134217728 | bytes 8929280 | tf_op jit(solution)/shard_map/dot_general | solution.py:86
  142.0 65.5 %all-reduce.2 = bf16[16,8192]{1,0:T(8,128)(2,1)S(1)} all-reduce(f32[16,8192]{1,0:T(8,128)S(1)} %fusion.5), channel_id=2, replica_groups=mesh['groups'=2,'dp'=16] {'dp'}, use_global_device_ids=true, to_apply=%region_9.10.clone | all-reduce | flops 131072 | bytes 786432
  207.5 1.3 dynamic-slice_convert_fusion
  (24 shorter events, 0.1 us)
Async XLA Ops:
  5.8 7.5 %copy-start.5 = (s32[8,2]{0,1:T(2,128)S(1)}, s32[8,2]{0,1:T(2,128)}, u32[]{:S(2)}) copy-start(s32[8,2]{0,1:T(2,128)} %param.25) | copy-start | bytes 196
  5.9 48.5 %all-to-all-start = ((bf16[1,128,64,128]{3,2,0,1:T(8,128)(2,1)}), bf16[1,128,64,128]{3,2,0,1:T(8,128)(2,1)S(1)}, u32[]{:S(2)}, u32[]{:S(2)}) async-start(bf16[1,128,64,128]{3,2,0,1:T(8,128)(2,1)} %bitcast_select_fusion.1), calls=%async_computation | async-start | bytes 4194304 | tf_op jit(solution)/shard_map/all_to_all | solution.py:60
  54.4 1.3 copy-start.1
  59.8 11.5 %copy-start.2 = (bf16[1,8192]{1,0:T(2,128)(2,1)S(1)}, bf16[1,8192]{1,0:T(2,128)(2,1)}, u32[]{:S(2)}) copy-start(bf16[1,8192]{1,0:T(2,128)(2,1)} %param.14) | copy-start | bytes 49156
  59.8 11.7 %copy-start.6 = (bf16[1,512]{1,0:T(2,128)(2,1)S(1)}, bf16[1,512]{1,0:T(2,128)(2,1)}, u32[]{:S(2)}) copy-start(bf16[1,512]{1,0:T(2,128)(2,1)} %param.16) | copy-start | bytes 3076
  59.8 11.7 %copy-start.7 = (bf16[1,512]{1,0:T(2,128)(2,1)S(1)}, bf16[1,512]{1,0:T(2,128)(2,1)}, u32[]{:S(2)}) copy-start(bf16[1,512]{1,0:T(2,128)(2,1)} %param.17) | copy-start | bytes 3076
  59.8 11.7 %copy-start.8 = (f32[128]{0:T(128)S(1)}, f32[128]{0:T(128)}, u32[]{:S(2)}) copy-start(f32[128]{0:T(128)} %param.21) | copy-start | bytes 1540
  59.9 16.4 %copy-start.12 = (u32[32]{0:T(128)S(1)}, u32[32]{0:T(128)}, u32[]{:S(2)}) copy-start(u32[32]{0:T(128)} %constant.78) | copy-start | bytes 388
  59.9 17.0 %copy-start.9 = (f32[128]{0:T(128)S(1)}, f32[128]{0:T(128)}, u32[]{:S(2)}) copy-start(f32[128]{0:T(128)} %param.20) | copy-start | bytes 1540
  59.9 17.0 %copy-start.10 = (f32[1,128]{1,0:T(1,128)S(1)}, f32[1,128]{1,0:T(1,128)}, u32[]{:S(2)}) copy-start(f32[1,128]{1,0:T(1,128)} %param.18) | copy-start | bytes 1540
  59.9 17.0 %copy-start.11 = (f32[128]{0:T(128)S(1)}, f32[128]{0:T(128)}, u32[]{:S(2)}) copy-start(f32[128]{0:T(128)} %param.19) | copy-start | bytes 1540
  59.9 52.5 %copy-start = (bf16[1,128,64,128]{3,2,1,0:T(8,128)(2,1)S(1)}, bf16[1,128,64,128]{3,2,1,0:T(8,128)(2,1)}, u32[]{:S(2)}) copy-start(bf16[1,128,64,128]{3,2,1,0:T(8,128)(2,1)} %param.13) | copy-start | bytes 6291460
  59.9 52.4 %all-to-all-start.1 = ((bf16[16,8,64,128]{3,2,1,0:T(8,128)(2,1)}), bf16[16,8,64,128]{3,2,1,0:T(8,128)(2,1)}, u32[]{:S(2)}, u32[]{:S(2)}) async-start(bf16[16,8,64,128]{3,2,1,0:T(8,128)(2,1)} %select_select_fusion), calls=%async_computation.1 | async-start | bytes 4194304 | tf_op jit(solution)/shard_map/all_to_all | solution.py:62
  112.4 3.8 %copy-start.4 = (bf16[1,8192]{1,0:T(2,128)(2,1)S(1)}, bf16[1,8192]{1,0:T(2,128)(2,1)}, u32[]{:S(2)}) copy-start(bf16[1,8192]{1,0:T(2,128)(2,1)} %param.15) | copy-start | bytes 49156
  112.4 4.3 %copy-start.3 = (f32[8192]{0:T(1024)S(1)}, f32[8192]{0:T(1024)}, u32[]{:S(2)}) copy-start(f32[8192]{0:T(1024)} %param.22) | copy-start | bytes 98308
  118.6 18.8 %all-to-all-start.2 = ((bf16[16,2,256]{2,1,0:T(2,128)(2,1)}), bf16[16,2,256]{2,1,0:T(2,128)(2,1)S(1)}, u32[]{:S(2)}, u32[]{:S(2)}) async-start(bf16[16,2,256]{2,1,0:T(2,128)(2,1)} %reshape.247), calls=%async_computation.2 | async-start | bytes 32768 | tf_op jit(solution)/shard_map/all_to_all | solution.py:84
where the time goes:
time: 209 us
  waiting for transfers between devices  77.8 us (37%)
  blocking collectives  65.5 us (31%)
  starting transfers between devices  31.2 us (15%)
  other arithmetic  18.2 us (9%)
  local copies, waits for them, and re-layouts  7.43 us (4%)
  matrix products  4.58 us (2%)
  between operations  4.07 us (2%)
    unnamed x1, blocking collectives  65.5 us
    all_to_all x1, waiting for transfers between devices, local(): lax.all_to_all(outgoing, 'dp', split_axis=1, concat_axis=0, tiled=True)  40.8 us
    all_to_all x1, waiting for transfers between devices, local(): lax.all_to_all(jnp.where(has_sender[:, None, None, None], routed, jnp.zer...  35.4 us
    all_to_all x1, starting transfers between devices, local(): lax.all_to_all(normed, 'dp', split_axis=1, concat_axis=0, tiled=True)  12.3 us
    all_to_all x1, starting transfers between devices, local(): lax.all_to_all(jnp.where(has_sender[:, None, None, None], routed, jnp.zer...  11.4 us
    all_to_all x1, starting transfers between devices, local(): lax.all_to_all(outgoing, 'dp', split_axis=1, concat_axis=0, tiled=True)  7.52 us
    unnamed x2, other arithmetic  5.57 us
    dot_general x1, matrix products, local(): jnp.dot(head_cols, out_proj, preferred_element_type=jnp.float32)  4.58 us
  transfers between devices with their start and end apart: 3, of which 3 were waited for; matrix products, arithmetic and copies ran while one was open for 4% of the time, Pallas kernels for 0%

commit v1 on v0

v1 whole, which is shorter than its diff:
```python
import functools

import jax
import jax.numpy as jnp
from jax import lax
from jax.experimental import pallas as pl
from jax.experimental.pallas import tpu as pltpu
from jax.sharding import PartitionSpec as P

AXIS = "dp"
LANES = 128
MOST_PATTERNS = 32
F32 = jnp.float32
BF16 = jnp.bfloat16


def pair_switch(index, devices, array):
    def branch(distance, low_sends):
        pairs = [(i, i ^ distance) for i in range(devices) if (i < (i ^ distance)) == low_sends]
        return lambda a: lax.ppermute(a, AXIS, pairs)

    branches = [branch(d, low) for d in range(1, devices) for low in (True, False)]
    return lax.switch(index, branches, array)


def spread_and_collect(state, source, target, devices):
    ids = jnp.arange(devices, dtype=jnp.int32)
    matches = target[:, None] == ids[None, :]
    sender_of = jnp.sum(jnp.where(matches, source[:, None], 0), axis=0)
    has_sender = jnp.any(matches, axis=0)
    view = lax.all_to_all(state, AXIS, split_axis=1, concat_axis=0, tiled=True)
    routed = jnp.where(
        has_sender[:, None, None, None], jnp.take(view, sender_of, axis=0), jnp.zeros((), state.dtype)
    )
    return lax.all_to_all(routed, AXIS, split_axis=0, concat_axis=1, tiled=True)


def mix_kernel(live, s, x, z, b, c, per_head, gain, out):
    heads, p_size, n = s.shape
    width = heads * p_size
    c16 = jnp.broadcast_to(c[...], (16, n))
    t = lax.dot_general(
        c16, s[...].reshape(width, n), (((1,), (1,)), ((), ())), preferred_element_type=F32
    )[0:1]
    bc = jnp.sum(b[...].astype(F32) * c[...].astype(F32), axis=1, keepdims=True)
    xf = x[...].astype(F32)
    y = per_head[0:1] * t + (per_head[1:2] * xf) * bc + per_head[2:3] * xf
    gated = y * jax.nn.silu(z[...].astype(F32))
    factor = lax.rsqrt(jnp.mean(gated * gated, axis=1, keepdims=True) + 1e-05)
    normed = jnp.where(live[0] > 0, gated * factor * gain[...], 0.0)
    for q in range(width // LANES):
        out[q : q + 1, :] = normed[:, q * LANES : (q + 1) * LANES].astype(BF16)


def update_kernel(live, decay, s, x, b, per_head, out):
    heads, p_size, n = s.shape
    g = pl.program_id(0)
    dx = per_head[1:2] * x[...].astype(F32)
    first = dx.astype(BF16)
    rest = dx - first.astype(F32)
    second = rest.astype(BF16)
    third = (rest - second.astype(F32)).astype(BF16)
    row = lax.broadcasted_iota(jnp.int32, (16, dx.shape[1]), 0)
    terms = jnp.where(
        row == 0,
        first.astype(F32),
        jnp.where(row == 1, second.astype(F32), jnp.where(row == 2, third.astype(F32), 0.0)),
    ).astype(BF16)
    outer = lax.dot_general(
        terms, jnp.broadcast_to(b[...], (16, n)), (((0,), (0,)), ((), ())), preferred_element_type=F32
    )
    for h in range(heads):
        fresh = decay[g * heads + h] * s[h].astype(F32) + outer[h * p_size : (h + 1) * p_size]
        out[h] = jnp.where(live[0] > 0, fresh, 0.0).astype(BF16)


def project_kernel(rows, w, out):
    depth, lanes = rows.shape[1:]
    total = None
    for r in range(depth):
        part = jnp.dot(rows[:, r, :], w[r * lanes : (r + 1) * lanes, :], preferred_element_type=F32)
        total = part if total is None else total + part
    for j in range(w.shape[1] // LANES):
        out[:, j, :] = total[:, j * LANES : (j + 1) * LANES].astype(out.dtype)


def sum_kernel(parts, out):
    total = jnp.sum(parts[...].astype(F32), axis=0).astype(BF16)
    for q in range(total.shape[0]):
        out[0:1, q * LANES : (q + 1) * LANES] = total[q : q + 1, :]


def local(
    state,
    x_in,
    z_gate,
    b_in,
    c_in,
    dt_raw,
    dt_bias,
    a_log,
    d_skip,
    norm_gain,
    out_proj,
    active,
    plan,
):
    devices = lax.axis_size(AXIS)
    me = lax.axis_index(AXIS)
    heads, p_size, n = state.shape[1:]
    groups = b_in.shape[1] // n
    width = heads * p_size
    columns = out_proj.shape[1]
    source, target = plan[:, 0], plan[:, 1]
    partner = jnp.sum(jnp.where(source == me, target, 0) + jnp.where(target == me, source, 0))
    sends = jnp.any(source == me)
    live = jnp.where(sends, 0, 1).astype(jnp.int32).reshape(1)

    if 2 * (devices - 1) <= MOST_PATTERNS and devices & (devices - 1) == 0:
        low_sends = sends == (me < partner)
        index = 2 * ((me ^ partner) - 1) + jnp.where(low_sends, 0, 1)
        came = pair_switch(index, devices, state)
    else:
        came = spread_and_collect(state, source, target, devices)
    came = came.reshape(heads, p_size, n)

    step = jax.nn.softplus(dt_raw[0] + dt_bias)
    decay = jnp.exp(-jnp.exp(a_log) * step)
    per_head = jnp.repeat(jnp.stack([decay, step, d_skip]), p_size, axis=1)
    gain = norm_gain.reshape(1, width)

    smem = pl.BlockSpec(memory_space=pltpu.SMEM)
    of_group = width // groups
    state_spec = pl.BlockSpec((heads // groups, p_size, n), lambda g: (g, 0, 0))
    row_spec = pl.BlockSpec((1, of_group), lambda g: (0, g))
    n_spec = pl.BlockSpec((1, n), lambda g: (0, g))
    head_spec = pl.BlockSpec((3, of_group), lambda g: (0, g))

    normed = pl.pallas_call(
        mix_kernel,
        name="mix",
        grid=(groups,),
        in_specs=[smem, state_spec, row_spec, row_spec, n_spec, n_spec, head_spec, row_spec],
        out_specs=pl.BlockSpec((of_group // LANES, LANES), lambda g: (g, 0)),
        out_shape=jax.ShapeDtypeStruct((width // LANES, LANES), BF16),
    )(live, came, x_in, z_gate, b_in, c_in, per_head, gain)

    block = width // devices
    lanes = min(block, LANES)
    mine = lax.all_to_all(
        normed.reshape(devices, block // lanes, lanes), AXIS, split_axis=0, concat_axis=0, tiled=True
    )

    new_state = pl.pallas_call(
        update_kernel,
        name="update",
        grid=(groups,),
        in_specs=[smem, smem, state_spec, row_spec, n_spec, head_spec],
        out_specs=state_spec,
        out_shape=jax.ShapeDtypeStruct((heads, p_size, n), BF16),
    )(live, decay, came, x_in, b_in, per_head)

    tile = 1024
    partial = pl.pallas_call(
        project_kernel,
        name="project",
        grid=(columns // tile,),
        in_specs=[
            pl.BlockSpec((devices, block // lanes, lanes), lambda i: (0, 0, 0)),
            pl.BlockSpec((block, tile), lambda i: (0, i)),
        ],
        out_specs=pl.BlockSpec((devices, tile // LANES, LANES), lambda i: (0, i, 0)),
        out_shape=jax.ShapeDtypeStruct((devices, columns // LANES, LANES), F32),
    )(mine, out_proj)
    partial = lax.all_to_all(partial, AXIS, split_axis=0, concat_axis=0, tiled=True)
    mixed = pl.pallas_call(
        sum_kernel,
        name="total",
        out_shape=jax.ShapeDtypeStruct((1, columns), BF16),
    )(partial)
    return (mixed, new_state[None])


def solution(mesh):
    in_specs = (
        P(("groups", "dp"), None, None, None),
        P(("groups", "dp"), None),
        P(("groups", "dp"), None),
        P(("groups", "dp"), None),
        P(("groups", "dp"), None),
        P(("groups", "dp"), None),
        P(),
        P(),
        P(),
        P(),
        P("dp", None),
        P(("groups", "dp")),
        P("groups", None),
    )
    out_specs = (P(("groups", "dp"), None), P(("groups", "dp"), None, None, None))
    return jax.shard_map(local, mesh=mesh, in_specs=in_specs, out_specs=out_specs, check_vma=False)
```

time: 209 us -> 104 us (0.50)
  waiting for transfers between devices: 77.8 us -> 32.3 us
  blocking collectives: 65.5 us -> 31.7 us
  starting transfers between devices: 31.2 us -> 12.3 us
  Pallas kernels: 0 us -> 18 us
  other arithmetic: 18.2 us -> 4.09 us
  local copies, waits for them, and re-layouts: 7.43 us -> 1.73 us
  matrix products: 4.58 us -> 0 us
    all_to_all x3 -> x1, waiting for transfers between devices: 77.8 us -> 9.71 us  [local(): lax.all_to_all(partial, AXIS, split_axis=0, concat_axis=0, tiled=True)]
    unnamed x1 -> x0, blocking collectives: 65.5 us -> none
    all_to_all x0 -> x1, blocking collectives: none -> 31.7 us  [local(): lax.all_to_all(normed.reshape(devices, block // lanes, lanes), AXIS, spli...]
    all_to_all x3 -> x1, starting transfers between devices: 31.2 us -> 3.57 us  [local(): lax.all_to_all(partial, AXIS, split_axis=0, concat_axis=0, tiled=True)]
    ppermute x0 -> x1, waiting for transfers between devices: none -> 22.5 us  [branch(): return lambda a: lax.ppermute(a, AXIS, pairs)]
    pallas_call x0 -> x4, Pallas kernels: none -> 18 us  [the longest x1 7.55 us: local(): pl.pallas_call(project_kernel, name='project', grid=(columns // tile,), i...]
    ppermute x0 -> x1, starting transfers between devices: none -> 8.7 us  [branch(): return lambda a: lax.ppermute(a, AXIS, pairs)]
    unnamed x2 -> x0, other arithmetic: 5.57 us -> none
  transfers between devices with their start and end apart: 3 -> 2, of which waited for: 3 -> 2; matrix products, arithmetic and copies ran while one was open for 4% -> 0% of each run, Pallas kernels for 0% -> 4%
where the time goes in v1:
time: 104 us; the launch traced here: 103 us
  waiting for transfers between devices  32.3 us (31%)
  blocking collectives  31.7 us (30%)
  Pallas kernels  18 us (17%)
  starting transfers between devices  12.3 us (12%)
  other arithmetic  4.09 us (4%)
  between operations  3.26 us (3%)
  local copies, waits for them, and re-layouts  1.73 us (2%)
    all_to_all x1, blocking collectives, local(): lax.all_to_all(normed.reshape(devices, block // lanes, lanes), AXIS, spli...  31.7 us
    ppermute x1, waiting for transfers between devices, branch(): return lambda a: lax.ppermute(a, AXIS, pairs)  22.5 us
    all_to_all x1, waiting for transfers between devices, local(): lax.all_to_all(partial, AXIS, split_axis=0, concat_axis=0, tiled=True)  9.71 us
    ppermute x1, starting transfers between devices, branch(): return lambda a: lax.ppermute(a, AXIS, pairs)  8.7 us
    pallas_call x1, Pallas kernels, local(): pl.pallas_call(project_kernel, name='project', grid=(columns // tile,), i...  7.55 us
    pallas_call x1, Pallas kernels, local(): pl.pallas_call(update_kernel, name='update', grid=(groups,), in_specs=[sm...  4.53 us
    pallas_call x1, Pallas kernels, local(): pl.pallas_call(mix_kernel, name='mix', grid=(groups,), in_specs=[smem, st...  4.18 us
    all_to_all x1, starting transfers between devices, local(): lax.all_to_all(partial, AXIS, split_axis=0, concat_axis=0, tiled=True)  3.57 us
  transfers between devices with their start and end apart: 2, of which 2 were waited for; matrix products, arithmetic and copies ran while one was open for 0% of the time, Pallas kernels for 4%

profile of v1, /device:TPU:0, one launch (start us, length us, event | category | flops | bytes accessed | tf_op | source)
XLA Modules:
  0.0 103.3 jit_solution(1960592770989508515)
XLA Ops:
  0.6 1.4 %fusion.1 = s32[]{:T(128)} fusion(s32[8,2]{0,1:T(2,128)} %param.54, s32[]{:T(128)S(6)} %axis_index.12), kind=kLoop, calls=%fused_computation.8 | loop fusion | flops 47 | bytes 72 | tf_op jit(solution)/shard_map/reduce_sum | solution.py:115
  2.0 1.3 %compare_reduce_fusion = pred[]{:T(512)} fusion(s32[8,2]{0,1:T(2,128)} %param.54, s32[]{:T(128)S(6)} %axis_index.12), kind=kLoop, calls=%fused_computation.4 | loop fusion | flops 15 | bytes 37 | tf_op jit(solution)/shard_map/reduce_or | solution.py:116
  5.9 0.7 multiply_exponential_fusion
  6.6 0.0 copy-start.1
  6.7 0.7 pad_maximum_fusion
  7.3 0.1 broadcast_in_dim.12
  7.4 0.8 reshape.78.per_head
  8.2 31.2 %conditional.1 = (bf16[128,64,128]{2,1,0:T(8,128)(2,1)}) conditional(s32[]{:T(128)} %clamp.3, bf16[1,128,64,128]{3,2,1,0:T(8,128)(2,1)} %param.43, bf16[1,128,64,128]{3,2,1,0:T(8,128)(2,1)} %param.43, bf16[1,128,64,128]{3,2,1,0:T(8,128)(2,1)} %param.43, bf16[1,128,64,128]{3,2,1,0:T(8,128)(2,1)} %param.43, ...), branch_computations={%region_2.3_spmd, %region_3.4_spmd, %region_4.5_spmd, %region_5.6_... | conditional | bytes 8388656 | solution.py:23
  8.2 8.7 %collective-permute-start.28 = (bf16[1,128,64,128]{3,2,1,0:T(8,128)(2,1)}, bf16[1,128,64,128]{3,2,1,0:T(8,128)(2,1)}, u32[]{:S(2)}, u32[]{:S(2)}) collective-permute-start(bf16[1,128,64,128]{3,2,1,0:T(8,128)(2,1)} %param.28), channel_id=1, source_target_pairs={{0,15},{1,14},{2,13},{3,12},{4,11},{5,10},{6,9},{7,8},{16,31},{17,... | collective-permute-start | bytes 6291464 | tf_op jit(solution)/shard_map/cond/branch_28_fun/ppermute | solution.py:20
  16.9 22.5 %collective-permute-done.28 = bf16[1,128,64,128]{3,2,1,0:T(8,128)(2,1)} collective-permute-done((bf16[1,128,64,128]{3,2,1,0:T(8,128)(2,1)}, bf16[1,128,64,128]{3,2,1,0:T(8,128)(2,1)}, u32[]{:S(2)}, u32[]{:S(2)}) %collective-permute-start.28) | collective-permute-done | bytes 2097184 | tf_op jit(solution)/shard_map/cond/branch_28_fun/ppermute | solution.py:20
  39.5 4.2 %mix.1 = bf16[64,128]{1,0:T(8,128)(2,1)} custom-call(s32[1]{0:T(128)} %bitcast.31.live, bf16[128,64,128]{2,1,0:T(8,128)(2,1)} %get-tuple-element.66.s, bf16[1,8192]{1,0:T(2,128)(2,1)} %x.3, bf16[1,8192]{1,0:T(2,128)(2,1)} %z.1, bf16[1,512]{1,0:T(2,128)(2,1)} %b.3, bf16[1,512]{1,0:T(2,128)(2,1)} %c.1, f32[3,8192]{1,0:T(4,128)} %reshape.78.per_head, ...), custom_call_target="tpu_custom_call" | custom-call | tf_op jit(solution)/shard_map/mix/pallas_call | solution.py:139
  43.7 31.7 %all_to_all.10.rows = bf16[16,4,128]{2,1,0:T(4,128)(2,1)} all-to-all(bf16[16,4,128]{2,1,0:T(4,128)(2,1)} %bitcast.52), channel_id=1, replica_groups=mesh['groups'=2,'dp'=16] {'dp'}, dimensions={0} | all-to-all | bytes 32768 | tf_op jit(solution)/shard_map/all_to_all | solution.py:150
  75.4 7.5 %project.1 = f32[16,64,128]{2,1,0:T(8,128)} custom-call(bf16[16,4,128]{2,1,0:T(4,128)(2,1)} %all_to_all.10.rows, bf16[512,8192]{1,0:T(8,128)(2,1)} %w.1), custom_call_target="tpu_custom_call" | custom-call | tf_op jit(solution)/shard_map/project/pallas_call | solution.py:164
  82.9 0.0 copy-done.1
  82.9 3.6 %all-to-all-start.1 = ((f32[16,64,128]{2,1,0:T(8,128)}), f32[16,64,128]{2,1,0:T(8,128)S(1)}, u32[]{:S(2)}, u32[]{:S(2)}) async-start(f32[16,64,128]{2,1,0:T(8,128)} %project.1), calls=%async_computation.1 | async-start | bytes 1048576 | tf_op jit(solution)/shard_map/all_to_all | solution.py:175
  86.5 4.5 %update.1 = bf16[128,64,128]{2,1,0:T(8,128)(2,1)} custom-call(s32[1]{0:T(128)} %bitcast.31.live, f32[128]{0:T(128)} %copy-done.1, bf16[128,64,128]{2,1,0:T(8,128)(2,1)} %get-tuple-element.66.s, bf16[1,8192]{1,0:T(2,128)(2,1)} %x.3, bf16[1,512]{1,0:T(2,128)(2,1)} %b.3, f32[3,8192]{1,0:T(4,128)} %reshape.78.per_head), custom_call_target="tpu_custom_call" | custom-call | tf_op jit(solution)/shard_map/update/pallas_call | solution.py:154
  91.0 9.7 %all-to-all-done.1.parts = f32[16,64,128]{2,1,0:T(8,128)S(1)} async-done(((f32[16,64,128]{2,1,0:T(8,128)}), f32[16,64,128]{2,1,0:T(8,128)S(1)}, u32[]{:S(2)}, u32[]{:S(2)}) %all-to-all-start.1) | async-done | bytes 524320 | tf_op jit(solution)/shard_map/all_to_all | solution.py:175
  100.7 0.0 copy-start
  100.7 0.8 copy-done
  101.6 1.7 %total.1 = bf16[1,8192]{1,0:T(2,128)(2,1)} custom-call(f32[16,64,128]{2,1,0:T(8,128)} %copy-done), custom_call_target="tpu_custom_call" | custom-call | tf_op jit(solution)/shard_map/total/pallas_call | solution.py:176
Async XLA Ops:
  6.6 76.3 %copy-start.1 = (f32[128]{0:T(128)}, f32[128]{0:T(128)S(1)}, u32[]{:S(2)}) copy-start(f32[128]{0:T(128)S(1)} %get-tuple-element.64.decay) | copy-start | bytes 1540
  8.2 31.2 %collective-permute-start.28 = (bf16[1,128,64,128]{3,2,1,0:T(8,128)(2,1)}, bf16[1,128,64,128]{3,2,1,0:T(8,128)(2,1)}, u32[]{:S(2)}, u32[]{:S(2)}) collective-permute-start(bf16[1,128,64,128]{3,2,1,0:T(8,128)(2,1)} %param.28), channel_id=1, source_target_pairs={{0,15},{1,14},{2,13},{3,12},{4,11},{5,10},{6,9},{7,8},{16,31},{17,... | collective-permute-start | bytes 6291464 | tf_op jit(solution)/shard_map/cond/branch_28_fun/ppermute | solution.py:20
  82.9 17.8 %all-to-all-start.1 = ((f32[16,64,128]{2,1,0:T(8,128)}), f32[16,64,128]{2,1,0:T(8,128)S(1)}, u32[]{:S(2)}, u32[]{:S(2)}) async-start(f32[16,64,128]{2,1,0:T(8,128)} %project.1), calls=%async_computation.1 | async-start | bytes 1048576 | tf_op jit(solution)/shard_map/all_to_all | solution.py:175
  100.7 0.8 copy-start

commit v2 on v1

v2 whole, which is shorter than its diff:
```python
import functools

import jax
import jax.numpy as jnp
from jax import lax
from jax.experimental import pallas as pl
from jax.experimental.pallas import tpu as pltpu
from jax.sharding import PartitionSpec as P

AXIS = "dp"
LANES = 128
MOST_PATTERNS = 32
GRANT = 8 * 2**20
F32 = jnp.float32
BF16 = jnp.bfloat16


def pair_switch(index, devices, array, beside, operands):
    def branch(distance, low_sends):
        pairs = [(i, i ^ distance) for i in range(devices) if (i < (i ^ distance)) == low_sends]
        return lambda a, ops: (lax.ppermute(a, AXIS, pairs), beside(*ops))

    branches = [branch(d, low) for d in range(1, devices) for low in (True, False)]
    return lax.switch(index, branches, array, operands)


def index_kernel(me, plan, index, live):
    def move(k, found):
        partner, sends = found
        source, target = plan[0, k], plan[1, k]
        partner = jnp.where(source == me[0], target, jnp.where(target == me[0], source, partner))
        return partner, jnp.where(source == me[0], 1, sends)

    partner, sends = lax.fori_loop(0, plan.shape[1], move, (jnp.int32(0), jnp.int32(0)))
    low_sends = jnp.where(me[0] < partner, sends, 1 - sends)
    index[0] = 2 * (jnp.bitwise_xor(me[0], partner) - 1) + 1 - low_sends
    live[0] = 1 - sends


def spread_and_collect(state, source, target, devices):
    ids = jnp.arange(devices, dtype=jnp.int32)
    matches = target[:, None] == ids[None, :]
    sender_of = jnp.sum(jnp.where(matches, source[:, None], 0), axis=0)
    has_sender = jnp.any(matches, axis=0)
    view = lax.all_to_all(state, AXIS, split_axis=1, concat_axis=0, tiled=True)
    routed = jnp.where(
        has_sender[:, None, None, None], jnp.take(view, sender_of, axis=0), jnp.zeros((), state.dtype)
    )
    return lax.all_to_all(routed, AXIS, split_axis=0, concat_axis=1, tiled=True)


def mix_kernel(live, s, x, z, b, c, per_head, gain, w, out, held_w, sem):
    copy = pltpu.make_async_copy(w, held_w, sem)
    copy.start()
    heads, p_size, n = s.shape
    groups = b.shape[1] // n
    held = heads // groups
    width = held * p_size
    for g in range(groups):
        at = slice(g * width, (g + 1) * width)
        bg, cg = b[:, g * n : (g + 1) * n], c[:, g * n : (g + 1) * n]
        t = lax.dot_general(
            jnp.broadcast_to(cg, (16, n)),
            s[g * held : (g + 1) * held].reshape(width, n),
            (((1,), (1,)), ((), ())),
            preferred_element_type=F32,
        )[0:1]
        bc = jnp.sum(bg.astype(F32) * cg.astype(F32), axis=1, keepdims=True)
        xf = x[:, at].astype(F32)
        y = per_head[0:1, at] * t + (per_head[1:2, at] * xf) * bc + per_head[2:3, at] * xf
        gated = y * jax.nn.silu(z[:, at].astype(F32))
        factor = lax.rsqrt(jnp.mean(gated * gated, axis=1, keepdims=True) + 1e-05)
        normed = jnp.where(live[0] > 0, gated * factor * gain[:, at], 0.0).astype(BF16)
        for q in range(width // LANES):
            row = g * (width // LANES) + q
            out[row : row + 1, :] = normed[:, q * LANES : (q + 1) * LANES]
    copy.wait()


def update_kernel(live, decay, s, x, b, per_head, out):
    heads, p_size, n = out.shape
    g = pl.program_id(0)
    dx = per_head[1:2] * x[...].astype(F32)
    first = dx.astype(BF16)
    rest = dx - first.astype(F32)
    second = rest.astype(BF16)
    third = (rest - second.astype(F32)).astype(BF16)
    row = lax.broadcasted_iota(jnp.int32, (16, dx.shape[1]), 0)
    terms = jnp.where(
        row == 0,
        first.astype(F32),
        jnp.where(row == 1, second.astype(F32), jnp.where(row == 2, third.astype(F32), 0.0)),
    ).astype(BF16)
    outer = lax.dot_general(
        terms, jnp.broadcast_to(b[...], (16, n)), (((0,), (0,)), ((), ())), preferred_element_type=F32
    )
    for h in range(heads):
        at = g * heads + h
        fresh = decay[at] * s[at].astype(F32) + outer[h * p_size : (h + 1) * p_size]
        out[h] = jnp.where(live[0] > 0, fresh, 0.0).astype(BF16)


def project_kernel(rows, w, out):
    tile = out.shape[1] * LANES
    lhs = jnp.concatenate([rows[:, r, :] for r in range(rows.shape[1])], axis=1)
    at = pl.ds(pl.multiple_of(pl.program_id(0) * tile, tile), tile)
    total = jnp.dot(lhs, w[:, at], preferred_element_type=F32).astype(out.dtype)
    for j in range(tile // LANES):
        out[:, j, :] = total[:, j * LANES : (j + 1) * LANES]


def sum_kernel(parts, out):
    total = jnp.sum(parts[...].astype(F32), axis=0).astype(BF16)
    for q in range(total.shape[0]):
        out[0:1, q * LANES : (q + 1) * LANES] = total[q : q + 1, :]


def local(
    state,
    x_in,
    z_gate,
    b_in,
    c_in,
    dt_raw,
    dt_bias,
    a_log,
    d_skip,
    norm_gain,
    out_proj,
    active,
    plan,
):
    devices = lax.axis_size(AXIS)
    me = lax.axis_index(AXIS)
    heads, p_size, n = state.shape[1:]
    groups = b_in.shape[1] // n
    width = heads * p_size
    columns = out_proj.shape[1]
    source, target = plan[:, 0], plan[:, 1]
    smem = pl.BlockSpec(memory_space=pltpu.SMEM)
    index, live = pl.pallas_call(
        index_kernel,
        name="index",
        in_specs=[smem, smem],
        out_specs=(smem, smem),
        out_shape=(jax.ShapeDtypeStruct((1,), jnp.int32),) * 2,
    )(me.astype(jnp.int32).reshape(1), plan.T)

    def prepare(dt_raw, dt_bias, a_log, d_skip):
        step = jax.nn.softplus(dt_raw[0] + dt_bias)
        decay = jnp.exp(-jnp.exp(a_log) * step)
        return decay, jnp.repeat(jnp.stack([decay, step, d_skip]), p_size, axis=1)

    operands = (dt_raw, dt_bias, a_log, d_skip)

    if 2 * (devices - 1) <= MOST_PATTERNS and devices & (devices - 1) == 0:
        came, (decay, per_head) = pair_switch(index[0], devices, state, prepare, operands)
    else:
        came = spread_and_collect(state, source, target, devices)
        decay, per_head = prepare(*operands)
    came = came.reshape(heads, p_size, n)
    gain = norm_gain.reshape(1, width)

    of_group = width // groups
    row_spec = pl.BlockSpec((1, of_group), lambda g: (0, g))
    vmem = pl.BlockSpec(memory_space=pltpu.VMEM)
    in_vmem = functools.partial(pltpu.with_memory_space_constraint, memory_space=pltpu.VMEM)
    params = pltpu.CompilerParams(vmem_limit_bytes=GRANT)
    came = in_vmem(came)

    normed, weights = pl.pallas_call(
        mix_kernel,
        name="mix",
        in_specs=[smem] + [vmem] * 7 + [pl.BlockSpec(memory_space=pltpu.HBM)],
        out_specs=(vmem, vmem),
        out_shape=(
            jax.ShapeDtypeStruct((width // LANES, LANES), BF16),
            pltpu.VMEM(out_proj.shape, BF16),
        ),
        scratch_shapes=[pltpu.SemaphoreType.DMA],
        compiler_params=params,
    )(live, came, *[in_vmem(a) for a in (x_in, z_gate, b_in, c_in, per_head, gain)], pltpu.with_memory_space_constraint(out_proj, pltpu.HBM))

    block = width // devices
    lanes = min(block, LANES)
    mine = lax.all_to_all(
        normed.reshape(devices, block // lanes, lanes), AXIS, split_axis=0, concat_axis=0, tiled=True
    )

    new_state = pl.pallas_call(
        update_kernel,
        name="update",
        grid=(groups,),
        in_specs=[
            smem,
            smem,
            vmem,
            row_spec,
            pl.BlockSpec((1, n), lambda g: (0, g)),
            pl.BlockSpec((3, of_group), lambda g: (0, g)),
        ],
        out_specs=pl.BlockSpec((heads // groups, p_size, n), lambda g: (g, 0, 0)),
        out_shape=jax.ShapeDtypeStruct((heads, p_size, n), BF16),
        compiler_params=params,
    )(live, decay, came, x_in, b_in, per_head)

    tile = 1024
    partial = pl.pallas_call(
        project_kernel,
        name="project",
        grid=(columns // tile,),
        in_specs=[vmem, vmem],
        out_specs=pl.BlockSpec((devices, tile // LANES, LANES), lambda i: (0, i, 0)),
        out_shape=jax.ShapeDtypeStruct((devices, columns // LANES, LANES), BF16),
        compiler_params=params,
    )(in_vmem(mine), in_vmem(weights))
    partial = lax.all_to_all(partial, AXIS, split_axis=0, concat_axis=0, tiled=True)
    mixed = pl.pallas_call(
        sum_kernel,
        name="total",
        in_specs=[vmem],
        out_shape=jax.ShapeDtypeStruct((1, columns), BF16),
        compiler_params=params,
    )(in_vmem(partial))
    return (mixed, new_state[None])


def solution(mesh):
    in_specs = (
        P(("groups", "dp"), None, None, None),
        P(("groups", "dp"), None),
        P(("groups", "dp"), None),
        P(("groups", "dp"), None),
        P(("groups", "dp"), None),
        P(("groups", "dp"), None),
        P(),
        P(),
        P(),
        P(),
        P("dp", None),
        P(("groups", "dp")),
        P("groups", None),
    )
    out_specs = (P(("groups", "dp"), None), P(("groups", "dp"), None, None, None))
    return jax.shard_map(local, mesh=mesh, in_specs=in_specs, out_specs=out_specs, check_vma=False)
```

time: 104 us -> 90.4 us (0.87)
  starting transfers between devices: 12.3 us -> 4.82 us
  blocking collectives: 31.7 us -> 34 us
  other arithmetic: 4.09 us -> 1.91 us
  waiting for transfers between devices: 32.3 us -> 30.2 us
  between operations: 3.26 us -> 1.37 us
  local copies, waits for them, and re-layouts: 1.73 us -> 0.27 us
  Pallas kernels: 18 us -> 16.8 us
    ppermute x1, starting transfers between devices: 8.7 us -> 1.29 us  [branch(): return lambda a, ops: (lax.ppermute(a, AXIS, pairs), beside(*ops))]
    all_to_all x1, waiting for transfers between devices: 9.71 us -> 5 us  [local(): lax.all_to_all(partial, AXIS, split_axis=0, concat_axis=0, tiled=True)]
    pallas_call x1, Pallas kernels: 7.55 us -> 3.95 us  [local(): pl.pallas_call(project_kernel, name='project', grid=(columns // tile,), i...]
    ppermute x1, waiting for transfers between devices: 22.5 us -> 25.2 us  [branch(): return lambda a, ops: (lax.ppermute(a, AXIS, pairs), beside(*ops))]
    all_to_all x1, blocking collectives: 31.7 us -> 34 us  [local(): lax.all_to_all(normed.reshape(devices, block // lanes, lanes), AXIS, spli...]
    pallas_call x2 -> x3, Pallas kernels: 5.89 us -> 7.88 us  [the longest x1 5.92 us: local(): pl.pallas_call(mix_kernel, name='mix', in_specs=[smem] + [vmem] * 7 + [pl...]
    reduce_sum x1 -> x0, other arithmetic: 1.39 us -> none  [local(): jnp.sum(jnp.where(source == me, target, 0) + jnp.where(target == me, sour...]
    reduce_or x1 -> x0, other arithmetic: 1.32 us -> none  [local(): sends = jnp.any(source == me)]
  transfers between devices with their start and end apart: 2 -> 2, of which waited for: 2 -> 2; matrix products, arithmetic and copies ran while one was open for 0% -> 2% of each run, Pallas kernels for 4% -> 6%
where the time goes in v2:
time: 90.4 us; the launch traced here: 89.4 us
  blocking collectives  34 us (38%)
  waiting for transfers between devices  30.2 us (33%)
  Pallas kernels  16.8 us (19%)
  starting transfers between devices  4.82 us (5%)
  other arithmetic  1.91 us (2%)
  between operations  1.37 us (2%)
    all_to_all x1, blocking collectives, local(): lax.all_to_all(normed.reshape(devices, block // lanes, lanes), AXIS, spli...  34 us
    ppermute x1, waiting for transfers between devices, branch(): return lambda a, ops: (lax.ppermute(a, AXIS, pairs), beside(*ops))  25.2 us
    pallas_call x1, Pallas kernels, local(): pl.pallas_call(mix_kernel, name='mix', in_specs=[smem] + [vmem] * 7 + [pl...  5.92 us
    all_to_all x1, waiting for transfers between devices, local(): lax.all_to_all(partial, AXIS, split_axis=0, concat_axis=0, tiled=True)  5 us
    pallas_call x1, Pallas kernels, local(): pl.pallas_call(update_kernel, name='update', grid=(groups,), in_specs=[sm...  4.98 us
    pallas_call x1, Pallas kernels, local(): pl.pallas_call(project_kernel, name='project', grid=(columns // tile,), i...  3.95 us
    all_to_all x1, starting transfers between devices, local(): lax.all_to_all(partial, AXIS, split_axis=0, concat_axis=0, tiled=True)  3.53 us
  transfers between devices with their start and end apart: 2, of which 2 were waited for; matrix products, arithmetic and copies ran while one was open for 2% of the time, Pallas kernels for 6%

profile of v2, /device:TPU:0, one launch (start us, length us, event | category | flops | bytes accessed | tf_op | source)
XLA Modules:
  0.0 89.4 jit_solution(6658341439973072001)
XLA Ops:
  0.6 1.3 %index.1 = (s32[1]{0:T(128)}, s32[1]{0:T(128)}) custom-call(s32[1]{0:T(128)} %bitcast.150.me, s32[2,8]{1,0:T(2,128)} %bitcast.339), custom_call_target="tpu_custom_call" | custom-call | tf_op jit(solution)/shard_map/index/pallas_call | solution.py:141
  2.6 0.0 copy-start
  2.6 0.0 copy-start.1
  2.6 0.0 copy-start.2
  2.6 0.0 copy-start.3
  2.6 0.0 copy-start.4
  2.6 28.7 %conditional.1 = (f32[128]{0:T(128)}, f32[3,8192]{1,0:T(4,128)S(1)}, bf16[128,64,128]{2,1,0:T(8,128)(2,1)}) conditional(s32[]{:T(128)} %bitcast.152, (f32[128]{0:T(128)}, f32[1,128]{1,0:T(1,128)}, f32[128]{0:T(128)}, f32[128]{0:T(128)}, bf16[1,128,64,128]{3,2,1,0:T(8,128)(2,1)}) %tuple.158, (f32[128]{0:T(128)}, ...), branch_computations={%region_0.1_spmd, %region_1.2_spmd, %region_2.3_spmd, %region_3.4_... | conditional | flops 1920 | bytes 8690752 | solution.py:24
  2.7 1.3 %collective-permute-start.7 = (bf16[1,128,64,128]{3,2,1,0:T(8,128)(2,1)}, bf16[1,128,64,128]{3,2,1,0:T(8,128)(2,1)}, u32[]{:S(2)}, u32[]{:S(2)}) collective-permute-start(bf16[1,128,64,128]{3,2,1,0:T(8,128)(2,1)} %get-tuple-element.340), channel_id=1, source_target_pairs={{4,0},{5,1},{6,2},{7,3},{12,8},{13,9},{14,10},{15,11},{20,16},{21,... | collective-permute-start | bytes 6291464 | tf_op jit(solution)/shard_map/cond/branch_7_fun/ppermute | solution.py:21
  4.0 1.2 %multiply_exponential_fusion.7 = (f32[128]{0:T(128)}, f32[128]{0:T(128)S(1)}) fusion(f32[128]{0:T(128)} %get-tuple-element.336, f32[128]{0:T(128)} %get-tuple-element.338, f32[1,128]{1,0:T(1,128)} %get-tuple-element.337), kind=kLoop, calls=%fused_computation.31 | loop fusion | flops 1152 | bytes 2560 | tf_op jit(solution)/shard_map/cond/branch_7_fun/exp | solution.py:151
  5.2 0.7 pad_maximum_fusion.7
  5.9 0.1 broadcast_in_dim.69
  6.0 0.1 reshape.105
  6.1 25.2 %collective-permute-done.7 = bf16[1,128,64,128]{3,2,1,0:T(8,128)(2,1)} collective-permute-done((bf16[1,128,64,128]{3,2,1,0:T(8,128)(2,1)}, bf16[1,128,64,128]{3,2,1,0:T(8,128)(2,1)}, u32[]{:S(2)}, u32[]{:S(2)}) %collective-permute-start.7) | collective-permute-done | bytes 2097184 | tf_op jit(solution)/shard_map/cond/branch_7_fun/ppermute | solution.py:21
  31.3 0.0 copy-done
  31.3 0.0 copy-done.1
  31.3 0.0 copy-done.2
  31.3 0.0 copy-done.3
  31.3 0.0 copy-done.4
  31.4 5.9 %mix.1 = (bf16[64,128]{1,0:T(8,128)(2,1)S(1)}, bf16[512,8192]{1,0:T(8,128)(2,1)S(1)}) custom-call(s32[1]{0:T(128)} %get-tuple-element.460.live, bf16[128,64,128]{2,1,0:T(8,128)(2,1)} %get-tuple-element.462.s, bf16[1,8192]{1,0:T(2,128)(2,1)S(1)} %copy-done, bf16[1,8192]{1,0:T(2,128)(2,1)S(1)} %copy-done.1, bf16[1,512]{1,0:T(2,128)(2,1)S(1)} %copy-done.3, ...), custom_call_target="tpu_custom_call" | custom-call | tf_op jit(solution)/shard_map/mix/pallas_call | solution.py:171
  37.3 34.0 %all_to_all.10.rows = bf16[16,4,128]{2,1,0:T(4,128)(2,1)S(1)} all-to-all(bf16[16,4,128]{2,1,0:T(4,128)(2,1)S(1)} %bitcast.277), channel_id=1, replica_groups=mesh['groups'=2,'dp'=16] {'dp'}, dimensions={0} | all-to-all | bytes 32768 | tf_op jit(solution)/shard_map/all_to_all | solution.py:186
  71.2 3.9 %project.1 = bf16[16,64,128]{2,1,0:T(8,128)(2,1)} custom-call(bf16[16,4,128]{2,1,0:T(4,128)(2,1)S(1)} %all_to_all.10.rows, bf16[512,8192]{1,0:T(8,128)(2,1)S(1)} %get-tuple-element.465.w), custom_call_target="tpu_custom_call" | custom-call | tf_op jit(solution)/shard_map/project/pallas_call | solution.py:208
  75.2 3.5 %all-to-all-start.1 = ((bf16[16,64,128]{2,1,0:T(8,128)(2,1)}), bf16[16,64,128]{2,1,0:T(8,128)(2,1)S(1)}, u32[]{:S(2)}, u32[]{:S(2)}) async-start(bf16[16,64,128]{2,1,0:T(8,128)(2,1)} %project.1), calls=%async_computation.1 | async-start | bytes 524288 | tf_op jit(solution)/shard_map/all_to_all | solution.py:217
  78.7 5.0 %update.1 = bf16[128,64,128]{2,1,0:T(8,128)(2,1)} custom-call(s32[1]{0:T(128)} %get-tuple-element.460.live, f32[128]{0:T(128)} %get-tuple-element.466.decay, bf16[128,64,128]{2,1,0:T(8,128)(2,1)} %get-tuple-element.462.s, bf16[1,8192]{1,0:T(2,128)(2,1)S(1)} %copy-done, bf16[1,512]{1,0:T(2,128)(2,1)S(1)} %copy-done.3, f32[3,8192]{1,0:T(4,128)S(1)} %get-tuple-element.463.per_head), custom_call_target="tpu_custom_call" | custom-call | tf_op jit(solution)/shard_map/update/pallas_call | solution.py:190
  83.7 5.0 %all-to-all-done.1.parts = bf16[16,64,128]{2,1,0:T(8,128)(2,1)S(1)} async-done(((bf16[16,64,128]{2,1,0:T(8,128)(2,1)}), bf16[16,64,128]{2,1,0:T(8,128)(2,1)S(1)}, u32[]{:S(2)}, u32[]{:S(2)}) %all-to-all-start.1) | async-done | bytes 262176 | tf_op jit(solution)/shard_map/all_to_all | solution.py:217
  88.7 0.7 total.1
Async XLA Ops:
  2.6 28.8 %copy-start = (bf16[1,8192]{1,0:T(2,128)(2,1)S(1)}, bf16[1,8192]{1,0:T(2,128)(2,1)}, u32[]{:S(2)}) copy-start(bf16[1,8192]{1,0:T(2,128)(2,1)} %x.3) | copy-start | bytes 49156
  2.6 28.8 %copy-start.1 = (bf16[1,8192]{1,0:T(2,128)(2,1)S(1)}, bf16[1,8192]{1,0:T(2,128)(2,1)}, u32[]{:S(2)}) copy-start(bf16[1,8192]{1,0:T(2,128)(2,1)} %z.1) | copy-start | bytes 49156
  2.6 28.7 %copy-start.2 = (f32[8192]{0:T(1024)S(1)}, f32[8192]{0:T(1024)}, u32[]{:S(2)}) copy-start(f32[8192]{0:T(1024)} %param.52) | copy-start | bytes 98308
  2.6 28.7 %copy-start.3 = (bf16[1,512]{1,0:T(2,128)(2,1)S(1)}, bf16[1,512]{1,0:T(2,128)(2,1)}, u32[]{:S(2)}) copy-start(bf16[1,512]{1,0:T(2,128)(2,1)} %b.3) | copy-start | bytes 3076
  2.6 28.7 %copy-start.4 = (bf16[1,512]{1,0:T(2,128)(2,1)S(1)}, bf16[1,512]{1,0:T(2,128)(2,1)}, u32[]{:S(2)}) copy-start(bf16[1,512]{1,0:T(2,128)(2,1)} %c.1) | copy-start | bytes 3076
  2.7 28.7 %collective-permute-start.7 = (bf16[1,128,64,128]{3,2,1,0:T(8,128)(2,1)}, bf16[1,128,64,128]{3,2,1,0:T(8,128)(2,1)}, u32[]{:S(2)}, u32[]{:S(2)}) collective-permute-start(bf16[1,128,64,128]{3,2,1,0:T(8,128)(2,1)} %get-tuple-element.340), channel_id=1, source_target_pairs={{4,0},{5,1},{6,2},{7,3},{12,8},{13,9},{14,10},{15,11},{20,16},{21,... | collective-permute-start | bytes 6291464 | tf_op jit(solution)/shard_map/cond/branch_7_fun/ppermute | solution.py:21
  75.2 13.5 %all-to-all-start.1 = ((bf16[16,64,128]{2,1,0:T(8,128)(2,1)}), bf16[16,64,128]{2,1,0:T(8,128)(2,1)S(1)}, u32[]{:S(2)}, u32[]{:S(2)}) async-start(bf16[16,64,128]{2,1,0:T(8,128)(2,1)} %project.1), calls=%async_computation.1 | async-start | bytes 524288 | tf_op jit(solution)/shard_map/all_to_all | solution.py:217

commit v3 on v2

--- a/solution.py
+++ b/solution.py
@@ -10,7 +10,9 @@
 AXIS = "dp"
 LANES = 128
 MOST_PATTERNS = 32
-GRANT = 8 * 2**20
+TILE = 1024
+FIRST = 2
+GRANT = 16 * 2**20
 F32 = jnp.float32
 BF16 = jnp.bfloat16
 
@@ -49,32 +51,39 @@
     return lax.all_to_all(routed, AXIS, split_axis=0, concat_axis=1, tiled=True)
 
 
-def mix_kernel(live, s, x, z, b, c, per_head, gain, w, out, held_w, sem):
-    copy = pltpu.make_async_copy(w, held_w, sem)
-    copy.start()
-    heads, p_size, n = s.shape
-    groups = b.shape[1] // n
-    held = heads // groups
+def mix_kernel(live, s, x, z, b, c, per_head, gain, w, out, first_w, state, sems):
+    groups = b.shape[1] // s.shape[2]
+    held = s.shape[0] // groups
+    p_size, n = s.shape[1:]
     width = held * p_size
+    copies = [
+        pltpu.make_async_copy(s.at[pl.ds(g * held, held)], state.at[pl.ds(g * held, held)], sems.at[g])
+        for g in range(groups)
+    ]
+    copies.append(pltpu.make_async_copy(w.at[:, pl.ds(0, first_w.shape[1])], first_w, sems.at[groups]))
+    for copy in copies:
+        copy.start()
     for g in range(groups):
         at = slice(g * width, (g + 1) * width)
         bg, cg = b[:, g * n : (g + 1) * n], c[:, g * n : (g + 1) * n]
+        bc = jnp.sum(bg.astype(F32) * cg.astype(F32), axis=1, keepdims=True)
+        xf = x[:, at].astype(F32)
+        rest = (per_head[1:2, at] * xf) * bc + per_head[2:3, at] * xf
+        gate = jax.nn.silu(z[:, at].astype(F32))
+        copies[g].wait()
         t = lax.dot_general(
             jnp.broadcast_to(cg, (16, n)),
-            s[g * held : (g + 1) * held].reshape(width, n),
+            state[g * held : (g + 1) * held].reshape(width, n),
             (((1,), (1,)), ((), ())),
             preferred_element_type=F32,
         )[0:1]
-        bc = jnp.sum(bg.astype(F32) * cg.astype(F32), axis=1, keepdims=True)
-        xf = x[:, at].astype(F32)
-        y = per_head[0:1, at] * t + (per_head[1:2, at] * xf) * bc + per_head[2:3, at] * xf
-        gated = y * jax.nn.silu(z[:, at].astype(F32))
+        gated = (per_head[0:1, at] * t + rest) * gate
         factor = lax.rsqrt(jnp.mean(gated * gated, axis=1, keepdims=True) + 1e-05)
         normed = jnp.where(live[0] > 0, gated * factor * gain[:, at], 0.0).astype(BF16)
         for q in range(width // LANES):
             row = g * (width // LANES) + q
             out[row : row + 1, :] = normed[:, q * LANES : (q + 1) * LANES]
-    copy.wait()
+    copies[groups].wait()
 
 
 def update_kernel(live, decay, s, x, b, per_head, out):
@@ -95,18 +104,31 @@
         terms, jnp.broadcast_to(b[...], (16, n)), (((0,), (0,)), ((), ())), preferred_element_type=F32
     )
     for h in range(heads):
-        at = g * heads + h
-        fresh = decay[at] * s[at].astype(F32) + outer[h * p_size : (h + 1) * p_size]
+        fresh = decay[g * heads + h] * s[h].astype(F32) + outer[h * p_size : (h + 1) * p_size]
         out[h] = jnp.where(live[0] > 0, fresh, 0.0).astype(BF16)
 
 
-def project_kernel(rows, w, out):
-    tile = out.shape[1] * LANES
+def project_kernel(rows, first_w, w, out, rest_w, sems):
+    tiles = w.shape[1] // TILE
+    have = first_w.shape[1] // TILE
+    copies = [
+        pltpu.make_async_copy(
+            w.at[:, pl.ds((have + i) * TILE, TILE)], rest_w.at[:, pl.ds(i * TILE, TILE)], sems.at[i]
+        )
+        for i in range(tiles - have)
+    ]
+    for copy in copies:
+        copy.start()
     lhs = jnp.concatenate([rows[:, r, :] for r in range(rows.shape[1])], axis=1)
-    at = pl.ds(pl.multiple_of(pl.program_id(0) * tile, tile), tile)
-    total = jnp.dot(lhs, w[:, at], preferred_element_type=F32).astype(out.dtype)
-    for j in range(tile // LANES):
-        out[:, j, :] = total[:, j * LANES : (j + 1) * LANES]
+    for i in range(tiles):
+        if i < have:
+            weights = first_w[:, i * TILE : (i + 1) * TILE]
+        else:
+            copies[i - have].wait()
+            weights = rest_w[:, (i - have) * TILE : (i - have + 1) * TILE]
+        total = jnp.dot(lhs, weights, preferred_element_type=F32).astype(out.dtype)
+        for j in range(TILE // LANES):
+            out[:, i * (TILE // LANES) + j, :] = total[:, j * LANES : (j + 1) * LANES]
 
 
 def sum_kernel(parts, out):
@@ -166,20 +188,30 @@
     vmem = pl.BlockSpec(memory_space=pltpu.VMEM)
     in_vmem = functools.partial(pltpu.with_memory_space_constraint, memory_space=pltpu.VMEM)
     params = pltpu.CompilerParams(vmem_limit_bytes=GRANT)
-    came = in_vmem(came)
-
-    normed, weights = pl.pallas_call(
+    in_hbm = functools.partial(pltpu.with_memory_space_constraint, memory_space=pltpu.HBM)
+    hbm = pl.BlockSpec(memory_space=pltpu.HBM)
+    weights = in_hbm(out_proj)
+
+    normed, first_w = pl.pallas_call(
         mix_kernel,
         name="mix",
-        in_specs=[smem] + [vmem] * 7 + [pl.BlockSpec(memory_space=pltpu.HBM)],
+        in_specs=[smem, hbm] + [vmem] * 6 + [hbm],
         out_specs=(vmem, vmem),
         out_shape=(
             jax.ShapeDtypeStruct((width // LANES, LANES), BF16),
-            pltpu.VMEM(out_proj.shape, BF16),
+            pltpu.VMEM((out_proj.shape[0], FIRST * TILE), BF16),
         ),
-        scratch_shapes=[pltpu.SemaphoreType.DMA],
-        compiler_params=params,
-    )(live, came, *[in_vmem(a) for a in (x_in, z_gate, b_in, c_in, per_head, gain)], pltpu.with_memory_space_constraint(out_proj, pltpu.HBM))
+        scratch_shapes=[
+            pltpu.VMEM((heads, p_size, n), BF16),
+            pltpu.SemaphoreType.DMA((groups + 1,)),
+        ],
+        compiler_params=params,
+    )(
+        live,
+        in_hbm(came),
+        *[in_vmem(a) for a in (x_in, z_gate, b_in, c_in, per_head, gain)],
+        weights,
+    )
 
     block = width // devices
     lanes = min(block, LANES)
@@ -194,7 +226,7 @@
         in_specs=[
             smem,
             smem,
-            vmem,
+            pl.BlockSpec((heads // groups, p_size, n), lambda g: (g, 0, 0)),
             row_spec,
             pl.BlockSpec((1, n), lambda g: (0, g)),
             pl.BlockSpec((3, of_group), lambda g: (0, g)),
@@ -204,16 +236,18 @@
         compiler_params=params,
     )(live, decay, came, x_in, b_in, per_head)
 
-    tile = 1024
     partial = pl.pallas_call(
         project_kernel,
         name="project",
-        grid=(columns // tile,),
-        in_specs=[vmem, vmem],
-        out_specs=pl.BlockSpec((devices, tile // LANES, LANES), lambda i: (0, i, 0)),
+        in_specs=[vmem, vmem, hbm],
+        out_specs=vmem,
         out_shape=jax.ShapeDtypeStruct((devices, columns // LANES, LANES), BF16),
-        compiler_params=params,
-    )(in_vmem(mine), in_vmem(weights))
+        scratch_shapes=[
+            pltpu.VMEM((out_proj.shape[0], columns - FIRST * TILE), BF16),
+            pltpu.SemaphoreType.DMA((columns // TILE - FIRST,)),
+        ],
+        compiler_params=params,
+    )(in_vmem(mine), in_vmem(first_w), weights)
     partial = lax.all_to_all(partial, AXIS, split_axis=0, concat_axis=0, tiled=True)
     mixed = pl.pallas_call(
         sum_kernel,

time: 90.4 us -> 109 us (1.21)
  waiting for transfers between devices: 30.2 us -> 51.9 us
  Pallas kernels: 16.8 us -> 14.2 us
    ppermute x1, waiting for transfers between devices: 25.2 us -> 47.1 us  [branch(): return lambda a, ops: (lax.ppermute(a, AXIS, pairs), beside(*ops))]
    pallas_call x2, Pallas kernels: 9.87 us -> 7.14 us  [the longest x1 3.94 us: local(): pl.pallas_call(project_kernel, name='project', in_specs=[vmem, vmem, hbm]...]
  transfers between devices with their start and end apart: 2 -> 2, of which waited for: 2 -> 2; matrix products, arithmetic and copies ran while one was open for 2% -> 2% of each run, Pallas kernels for 6% -> 5%
where the time goes in v3:
time: 109 us; the launch traced here: 108 us
  waiting for transfers between devices  51.9 us (48%)
  blocking collectives  33.6 us (31%)
  Pallas kernels  14.2 us (13%)
  starting transfers between devices  4.83 us (4%)
  other arithmetic  1.91 us (2%)
  between operations  1.38 us (1%)
    ppermute x1, waiting for transfers between devices, branch(): return lambda a, ops: (lax.ppermute(a, AXIS, pairs), beside(*ops))  47.1 us
    all_to_all x1, blocking collectives, local(): lax.all_to_all(normed.reshape(devices, block // lanes, lanes), AXIS, spli...  33.6 us
    pallas_call x1, Pallas kernels, local(): pl.pallas_call(update_kernel, name='update', grid=(groups,), in_specs=[sm...  5.1 us
    all_to_all x1, waiting for transfers between devices, local(): lax.all_to_all(partial, AXIS, split_axis=0, concat_axis=0, tiled=True)  4.88 us
    pallas_call x1, Pallas kernels, local(): pl.pallas_call(project_kernel, name='project', in_specs=[vmem, vmem, hbm]...  3.94 us
    all_to_all x1, starting transfers between devices, local(): lax.all_to_all(partial, AXIS, split_axis=0, concat_axis=0, tiled=True)  3.54 us
    pallas_call x1, Pallas kernels, local(): pl.pallas_call(mix_kernel, name='mix', in_specs=[smem, hbm] + [vmem] * 6...  3.2 us
  transfers between devices with their start and end apart: 2, of which 2 were waited for; matrix products, arithmetic and copies ran while one was open for 2% of the time, Pallas kernels for 5%

profile of v3, /device:TPU:0, one launch (start us, length us, event | category | flops | bytes accessed | tf_op | source)
XLA Modules:
  0.0 108.2 jit_solution(4390894885982026710)
XLA Ops:
  0.6 1.3 %index.1 = (s32[1]{0:T(128)}, s32[1]{0:T(128)}) custom-call(s32[1]{0:T(128)} %bitcast.150.me, s32[2,8]{1,0:T(2,128)} %bitcast.339), custom_call_target="tpu_custom_call" | custom-call | tf_op jit(solution)/shard_map/index/pallas_call | solution.py:163
  2.6 0.0 copy-start
  2.6 0.0 copy-start.1
  2.6 0.0 copy-start.2
  2.6 0.0 copy-start.3
  2.6 0.0 copy-start.4
  2.6 50.6 %conditional.1 = (f32[128]{0:T(128)}, f32[3,8192]{1,0:T(4,128)S(1)}, bf16[128,64,128]{2,1,0:T(8,128)(2,1)}) conditional(s32[]{:T(128)} %bitcast.152, (f32[128]{0:T(128)}, f32[1,128]{1,0:T(1,128)}, f32[128]{0:T(128)}, f32[128]{0:T(128)}, bf16[1,128,64,128]{3,2,1,0:T(8,128)(2,1)}) %tuple.158, (f32[128]{0:T(128)}, ...), branch_computations={%region_0.1_spmd, %region_1.2_spmd, %region_2.3_spmd, %region_3.4_... | conditional | flops 1920 | bytes 8690752 | solution.py:26
  2.7 1.3 %collective-permute-start.25 = (bf16[1,128,64,128]{3,2,1,0:T(8,128)(2,1)}, bf16[1,128,64,128]{3,2,1,0:T(8,128)(2,1)}, u32[]{:S(2)}, u32[]{:S(2)}) collective-permute-start(bf16[1,128,64,128]{3,2,1,0:T(8,128)(2,1)} %get-tuple-element.430), channel_id=1, source_target_pairs={{8,5},{9,4},{10,7},{11,6},{12,1},{13,0},{14,3},{15,2},{24,21},{25,... | collective-permute-start | bytes 6291464 | tf_op jit(solution)/shard_map/cond/branch_25_fun/ppermute | solution.py:23
  4.0 1.2 %multiply_exponential_fusion.25 = (f32[128]{0:T(128)}, f32[128]{0:T(128)S(1)}) fusion(f32[128]{0:T(128)} %get-tuple-element.426, f32[128]{0:T(128)} %get-tuple-element.428, f32[1,128]{1,0:T(1,128)} %get-tuple-element.427), kind=kLoop, calls=%fused_computation.103 | loop fusion | flops 1152 | bytes 2560 | tf_op jit(solution)/shard_map/cond/branch_25_fun/exp | solution.py:173
  5.2 0.7 pad_maximum_fusion.25
  5.9 0.1 broadcast_in_dim.87
  6.0 0.1 reshape.154
  6.2 47.1 %collective-permute-done.25 = bf16[1,128,64,128]{3,2,1,0:T(8,128)(2,1)} collective-permute-done((bf16[1,128,64,128]{3,2,1,0:T(8,128)(2,1)}, bf16[1,128,64,128]{3,2,1,0:T(8,128)(2,1)}, u32[]{:S(2)}, u32[]{:S(2)}) %collective-permute-start.25) | collective-permute-done | bytes 2097184 | tf_op jit(solution)/shard_map/cond/branch_25_fun/ppermute | solution.py:23
  53.2 0.0 copy-done
  53.2 0.0 copy-done.1
  53.2 0.0 copy-done.2
  53.2 0.0 copy-done.3
  53.2 0.0 copy-done.4
  53.2 3.2 %mix.1 = (bf16[64,128]{1,0:T(8,128)(2,1)S(1)}, bf16[512,2048]{1,0:T(8,128)(2,1)S(1)}) custom-call(s32[1]{0:T(128)} %get-tuple-element.460.live, bf16[128,64,128]{2,1,0:T(8,128)(2,1)} %get-tuple-element.462.s, bf16[1,8192]{1,0:T(2,128)(2,1)S(1)} %copy-done, bf16[1,8192]{1,0:T(2,128)(2,1)S(1)} %copy-done.1, bf16[1,512]{1,0:T(2,128)(2,1)S(1)} %copy-done.3, ...), custom_call_target="tpu_custom_call" | custom-call | tf_op jit(solution)/shard_map/mix/pallas_call | solution.py:195
  56.5 33.6 %all_to_all.10.rows = bf16[16,4,128]{2,1,0:T(4,128)(2,1)S(1)} all-to-all(bf16[16,4,128]{2,1,0:T(4,128)(2,1)S(1)} %bitcast.277), channel_id=1, replica_groups=mesh['groups'=2,'dp'=16] {'dp'}, dimensions={0} | all-to-all | bytes 32768 | tf_op jit(solution)/shard_map/all_to_all | solution.py:218
  90.1 3.9 %project.1 = bf16[16,64,128]{2,1,0:T(8,128)(2,1)} custom-call(bf16[16,4,128]{2,1,0:T(4,128)(2,1)S(1)} %all_to_all.10.rows, bf16[512,2048]{1,0:T(8,128)(2,1)S(1)} %get-tuple-element.465.first_w, bf16[512,8192]{1,0:T(8,128)(2,1)} %w.3), custom_call_target="tpu_custom_call" | custom-call | tf_op jit(solution)/shard_map/project/pallas_call | solution.py:239
  94.0 3.5 %all-to-all-start.1 = ((bf16[16,64,128]{2,1,0:T(8,128)(2,1)}), bf16[16,64,128]{2,1,0:T(8,128)(2,1)S(1)}, u32[]{:S(2)}, u32[]{:S(2)}) async-start(bf16[16,64,128]{2,1,0:T(8,128)(2,1)} %project.1), calls=%async_computation.1 | async-start | bytes 524288 | tf_op jit(solution)/shard_map/all_to_all | solution.py:251
  97.6 5.1 %update.1 = bf16[128,64,128]{2,1,0:T(8,128)(2,1)} custom-call(s32[1]{0:T(128)} %get-tuple-element.460.live, f32[128]{0:T(128)} %get-tuple-element.466.decay, bf16[128,64,128]{2,1,0:T(8,128)(2,1)} %get-tuple-element.462.s, bf16[1,8192]{1,0:T(2,128)(2,1)S(1)} %copy-done, bf16[1,512]{1,0:T(2,128)(2,1)S(1)} %copy-done.3, f32[3,8192]{1,0:T(4,128)S(1)} %get-tuple-element.463.per_head), custom_call_target="tpu_custom_call" | custom-call | tf_op jit(solution)/shard_map/update/pallas_call | solution.py:222
  102.7 4.9 %all-to-all-done.1.parts = bf16[16,64,128]{2,1,0:T(8,128)(2,1)S(1)} async-done(((bf16[16,64,128]{2,1,0:T(8,128)(2,1)}), bf16[16,64,128]{2,1,0:T(8,128)(2,1)S(1)}, u32[]{:S(2)}, u32[]{:S(2)}) %all-to-all-start.1) | async-done | bytes 262176 | tf_op jit(solution)/shard_map/all_to_all | solution.py:251
  107.5 0.7 total.1
Async XLA Ops:
  2.6 50.6 %copy-start = (bf16[1,8192]{1,0:T(2,128)(2,1)S(1)}, bf16[1,8192]{1,0:T(2,128)(2,1)}, u32[]{:S(2)}) copy-start(bf16[1,8192]{1,0:T(2,128)(2,1)} %x.3) | copy-start | bytes 49156
  2.6 50.6 %copy-start.1 = (bf16[1,8192]{1,0:T(2,128)(2,1)S(1)}, bf16[1,8192]{1,0:T(2,128)(2,1)}, u32[]{:S(2)}) copy-start(bf16[1,8192]{1,0:T(2,128)(2,1)} %z.1) | copy-start | bytes 49156
  2.6 50.6 %copy-start.2 = (f32[8192]{0:T(1024)S(1)}, f32[8192]{0:T(1024)}, u32[]{:S(2)}) copy-start(f32[8192]{0:T(1024)} %param.52) | copy-start | bytes 98308
  2.6 50.6 %copy-start.3 = (bf16[1,512]{1,0:T(2,128)(2,1)S(1)}, bf16[1,512]{1,0:T(2,128)(2,1)}, u32[]{:S(2)}) copy-start(bf16[1,512]{1,0:T(2,128)(2,1)} %b.3) | copy-start | bytes 3076
  2.6 50.6 %copy-start.4 = (bf16[1,512]{1,0:T(2,128)(2,1)S(1)}, bf16[1,512]{1,0:T(2,128)(2,1)}, u32[]{:S(2)}) copy-start(bf16[1,512]{1,0:T(2,128)(2,1)} %c.1) | copy-start | bytes 3076
  2.7 50.5 %collective-permute-start.25 = (bf16[1,128,64,128]{3,2,1,0:T(8,128)(2,1)}, bf16[1,128,64,128]{3,2,1,0:T(8,128)(2,1)}, u32[]{:S(2)}, u32[]{:S(2)}) collective-permute-start(bf16[1,128,64,128]{3,2,1,0:T(8,128)(2,1)} %get-tuple-element.430), channel_id=1, source_target_pairs={{8,5},{9,4},{10,7},{11,6},{12,1},{13,0},{14,3},{15,2},{24,21},{25,... | collective-permute-start | bytes 6291464 | tf_op jit(solution)/shard_map/cond/branch_25_fun/ppermute | solution.py:23
  94.0 13.5 %all-to-all-start.1 = ((bf16[16,64,128]{2,1,0:T(8,128)(2,1)}), bf16[16,64,128]{2,1,0:T(8,128)(2,1)S(1)}, u32[]{:S(2)}, u32[]{:S(2)}) async-start(bf16[16,64,128]{2,1,0:T(8,128)(2,1)} %project.1), calls=%async_computation.1 | async-start | bytes 524288 | tf_op jit(solution)/shard_map/all_to_all | solution.py:251
